TPU v7x, 32 devices: a whole 2x2x4 slice. The times are simulated.
32 devices in a mesh: tp: 4 (over y, x), row: 4 (over z), col: 2 (over core).
Axes of the slice: x: 2, y: 2, z: 4, core: 2. Of those that a mesh axis runs over, the one named last changes fastest.
Arguments:
- hidden: bfloat16 [128, 14336], P('col', 'row'), may hold values from -6 to 6
- out_grad: bfloat16 [128, 4096], P(None, ('tp', 'row')), may hold values from -6 to 6
- basis_in: bfloat16 [14336, 4096], P(('row', 'col'), 'tp'), may hold values from -0.046875 to 0.046875
- basis_out: bfloat16 [4096, 1024], P(('tp', 'row'), 'col'), may hold values from -0.09375 to 0.09375
- eigen: float32 [4096, 1024], P(('tp', 'row'), 'col'), may hold values from 0.02 to 2
Outputs:
- precond: float32 [4096, 14336], P(('tp', 'col'), 'row')
All inputs are finite; a program needn't handle non-finite values.
Results may differ from a plain program's by a relative error of at most 0.024.
Values may be sent and summed in bfloat16 or wider, within the bound.
No kernel may reach another device: no remote copies, remote signals or barrier semaphores. Data moves between devices by JAX's collectives and lax.ppermute only.
A program may use at most 64 MiB of HBM per device.

v0:
```python
import jax
import jax.numpy as jnp
from jax import lax
from jax.sharding import PartitionSpec as P

damping = 0.01


def contract_rows(left, right):
    return lax.dot_general(
        left, right, (((0,), (0,)), ((), ())), preferred_element_type=jnp.float32
    )


def contract_cols(left, right):
    return lax.dot_general(
        left, right, (((1,), (1,)), ((), ())), preferred_element_type=jnp.float32
    )


def shards(hidden, out_grad, basis_in, basis_out, eigen):
    tp_count = lax.axis_size("tp")
    col_count = lax.axis_size("col")
    basis_block = lax.all_gather(basis_in, "col", axis=0, tiled=True)
    partial_in = jnp.dot(hidden, basis_block, preferred_element_type=jnp.float32)
    rotated_in = lax.psum_scatter(
        partial_in.astype(jnp.bfloat16), "row", scatter_dimension=1, tiled=True
    )
    rotated_in = lax.all_gather(rotated_in, "col", axis=0, tiled=True)
    queries = rotated_in.shape[0]
    partial_out = jnp.dot(out_grad, basis_out, preferred_element_type=jnp.float32)
    rotated_out = lax.psum(partial_out, ("tp", "row")).astype(jnp.bfloat16)
    coeff = contract_rows(rotated_in, rotated_out)
    scaled = (coeff / (queries * (eigen + damping))).astype(jnp.bfloat16)
    mixed_part = contract_cols(scaled, lax.all_gather(basis_out, ("tp", "row"), axis=0, tiled=True))
    depth = mixed_part.shape[0]
    width = mixed_part.shape[1]
    mixed_part = mixed_part.reshape(depth, tp_count, col_count, width // (tp_count * col_count))
    mixed = lax.psum_scatter(
        mixed_part.astype(jnp.bfloat16), "col", scatter_dimension=2, tiled=True
    ).astype(jnp.float32)
    mixed = mixed.reshape(depth, width // col_count).astype(jnp.bfloat16)
    mixed = lax.all_gather(mixed, "row", axis=0, tiled=True)
    return lax.psum_scatter(
        lax.dot_general(
            mixed, basis_block, (((0,), (1,)), ((), ())), preferred_element_type=jnp.float32
        ).astype(jnp.bfloat16),
        "tp",
        scatter_dimension=0,
        tiled=True,
    ).astype(jnp.float32)


def solution(mesh):
    placed = (
        P("col", "row"),
        P(None, ("tp", "row")),
        P(("row", "col"), "tp"),
        P(("tp", "row"), "col"),
        P(("tp", "row"), "col"),
    )
    return jax.shard_map(
        shards, mesh=mesh, in_specs=placed, out_specs=P(("tp", "col"), "row"), check_vma=False
    )
```

profile of v0, /device:TPU:0, one launch (start us, length us, event | category | flops | bytes accessed | tf_op | source)
XLA Modules:
  0.0 397.8 jit_solution(9604397828768367093)
XLA Ops:
  7.4 0.7 all-gather.4.cloned.1.call-update
  8.1 0.0 reduce-scatter.4.cloned.1.call-start
  8.2 22.6 %all-gather.4.cloned.1.call-done = bf16[3584,1024]{1,0:T(8,128)(2,1)} async-done(((bf16[1792,1024]{1,0:T(8,128)(2,1)}), bf16[3584,1024]{1,0:T(8,128)(2,1)}) %all-gather.4.cloned.1.call-update) | async-done | bytes 7340048 | tf_op jit(solution)/shard_map/all_gather | solution.py:24
  30.8 5.1 %convolution_convert_fusion.2 = bf16[64,1024]{1,0:T(8,128)(2,1)} fusion(bf16[64,3584]{1,0:T(8,128)(2,1)S(1)} %copy-done, bf16[3584,1024]{1,0:T(8,128)(2,1)} %all-gather.4.cloned.1.call-done), kind=kOutput, calls=%fused_computation.4 | convolution fusion | flops 469827584 | bytes 7929856 | tf_op jit(solution)/shard_map/dot_general | solution.py:25
  35.9 0.0 reduce-scatter.4.cloned.1.call-update
  35.9 0.0 all-gather.6.cloned.1.call-start
  36.0 0.5 all-gather.6.cloned.1.call-update
  36.5 0.0 reduce-scatter.6.cloned.1.call-start
  36.6 0.2 fusion.9
  36.8 85.1 %all-reduce.1 = bf16[128,512]{1,0:T(8,128)(2,1)S(1)} all-reduce(f32[128,512]{1,0:T(8,128)S(1)} %fusion.9), channel_id=1, replica_groups=mesh['tp'=4,'row'=4,'col'=2] {'tp','row'}, use_global_device_ids=true, to_apply=%region_1.0 | all-reduce | flops 65536 | bytes 393216 | tf_op jit(solution)/shard_map/psum | solution.py:32
  121.9 0.0 reduce-scatter.4.cloned.1.call-done
  121.9 2.1 all_gather.13
  124.0 4.9 %convolution_convert_fusion.1 = bf16[256,4096]{1,0:T(8,128)(2,1)} fusion(bf16[4096,512]{1,0:T(8,128)(2,1)} %all-gather.6.cloned.1.call-done, bf16[128,256]{1,0:T(8,128)(2,1)S(1)} %all_gather.13, f32[256,512]{1,0:T(8,128)S(1)} %copy-done.3, bf16[128,512]{1,0:T(8,128)(2,1)S(1)} %all-reduce.1), kind=kOutput, calls=%fused_computation.1 | convolution fusion | flops 1108869120 | bytes 7012352 | tf_op jit(solution)/shard_map/dot_general | solution.py:16
  128.9 3.3 convert_element_type.30
  132.2 4.1 %copy.6 = bf16[256,4,2,512]{0,3,1,2:T(8,128)(2,1)} copy(bf16[256,4,2,512]{3,2,1,0:T(2,128)(2,1)S(1)} %convert_element_type.30) | data formatting | bytes 4194304 | tf_op jit(solution)/shard_map/convert_element_type | solution.py:40
  136.3 0.0 reduce-scatter.6.cloned.1.call-update
  136.4 0.0 all-gather.8.cloned.1.call-start
  136.4 6.9 %reduce-scatter.6.cloned.1.call-done = bf16[256,4,1,512]{0,3,1,2:T(8,128)(2,1)} async-done(((bf16[256,4,2,512]{0,3,1,2:T(8,128)(2,1)}), bf16[256,4,1,512]{0,3,1,2:T(8,128)(2,1)}) %reduce-scatter.6.cloned.1.call-update) | async-done | bytes 1048592 | tf_op jit(solution)/shard_map/reduce_scatter | solution.py:39
  143.4 0.0 reduce-scatter.8.cloned.1.call-start
  143.4 83.2 %all-gather.8.cloned.1.call-done = bf16[1024,2048]{0,1:T(8,128)(2,1)} async-done(((bf16[256,2048]{0,1:T(8,128)(2,1)}), bf16[1024,2048]{0,1:T(8,128)(2,1)}) %all-gather.8.cloned.1.call-update) | async-done | bytes 4194320 | tf_op jit(solution)/shard_map/all_gather | solution.py:43
  226.6 22.0 %convolution_convert_fusion = bf16[2048,3584]{1,0:T(8,128)(2,1)} fusion(bf16[1024,2048]{0,1:T(8,128)(2,1)} %all-gather.8.cloned.1.call-done, bf16[3584,1024]{1,0:T(8,128)(2,1)} %all-gather.4.cloned.1.call-done), kind=kOutput, calls=%fused_computation | convolution fusion | flops 15039725568 | bytes 26214400 | tf_op jit(solution)/shard_map/dot_general | solution.py:45
  248.6 0.0 reduce-scatter.8.cloned.1.call-update
  248.7 135.9 %reduce-scatter.8.cloned.1.call-done = bf16[512,3584]{1,0:T(8,128)(2,1)} async-done(((bf16[2048,3584]{1,0:T(8,128)(2,1)}), bf16[512,3584]{1,0:T(8,128)(2,1)}) %reduce-scatter.8.cloned.1.call-update) | async-done | bytes 3670032 | tf_op jit(solution)/shard_map/reduce_scatter | solution.py:44
  384.6 6.0 %convert_element_type.33 = f32[512,3584]{1,0:T(8,128)} convert(bf16[512,3584]{1,0:T(8,128)(2,1)} %reduce-scatter.8.cloned.1.call-done) | non-fusion elementwise | flops 1835008 | bytes 11010048 | tf_op jit(solution)/shard_map/convert_element_type | solution.py:51
  (11 shorter events, 0.0 us)
Async XLA Ops:
  7.4 23.4 %copy-start = (bf16[64,3584]{1,0:T(8,128)(2,1)S(1)}, bf16[64,3584]{1,0:T(8,128)(2,1)}, u32[]{:S(2)}) copy-start(bf16[64,3584]{1,0:T(8,128)(2,1)} %param.5) | copy-start | bytes 1376260
  7.4 23.4 %all-gather.4.cloned.1.call-start = ((), (), s32[]{:S(2)}) async-start(), calls=%async_computation.3 | async-start | bytes 11010048 | tf_op jit(solution)/shard_map/all_gather | solution.py:24
  8.1 28.5 %copy-start.1 = (bf16[256,512]{1,0:T(8,128)(2,1)S(1)}, bf16[256,512]{1,0:T(8,128)(2,1)}, u32[]{:S(2)}) copy-start(bf16[256,512]{1,0:T(8,128)(2,1)} %param.8) | copy-start | bytes 786436
  8.1 28.5 %copy-start.2 = (bf16[128,256]{1,0:T(8,128)(2,1)S(1)}, bf16[128,256]{1,0:T(8,128)(2,1)}, u32[]{:S(2)}) copy-start(bf16[128,256]{1,0:T(8,128)(2,1)} %param.6) | copy-start | bytes 196612
  8.1 115.9 %copy-start.3 = (f32[256,512]{1,0:T(8,128)S(1)}, f32[256,512]{1,0:T(8,128)}, u32[]{:S(2)}) copy-start(f32[256,512]{1,0:T(8,128)} %param.9) | copy-start | bytes 1572868
  8.1 113.8 %reduce-scatter.4.cloned.1.call-start = ((), (), s32[]{:S(2)}) async-start(), calls=%async_computation.4 | async-start | bytes 163840 | tf_op jit(solution)/shard_map/reduce_scatter | solution.py:26
  35.9 88.1 %all-gather.6.cloned.1.call-start = ((), (), s32[]{:S(2)}) async-start(), calls=%async_computation.5 | async-start | bytes 4456448 | tf_op jit(solution)/shard_map/all_gather | solution.py:35
  36.5 106.8 %reduce-scatter.6.cloned.1.call-start = ((), (), s32[]{:S(2)}) async-start(), calls=%async_computation.6 | async-start | bytes 3145728 | tf_op jit(solution)/shard_map/reduce_scatter | solution.py:39
  136.4 90.2 %all-gather.8.cloned.1.call-start = ((), (), s32[]{:S(2)}) async-start(), calls=%async_computation.7 | async-start | bytes 5242880 | tf_op jit(solution)/shard_map/all_gather | solution.py:43
  143.4 241.2 %reduce-scatter.8.cloned.1.call-start = ((), (), s32[]{:S(2)}) async-start(), calls=%async_computation.8 | async-start | bytes 18350080 | tf_op jit(solution)/shard_map/reduce_scatter | solution.py:44
Sparse Core Ops, SparseCore 0:
  9.7 21.0 all-gather.3
  36.0 21.2 reduce-scatter.3
  136.5 6.8 reduce-scatter.5
  144.7 81.7 all-gather.7
Sparse Core Ops, SparseCore 1:
  39.2 78.1 all-gather.5
  248.7 135.8 reduce-scatter.7
where the time goes:
time: 398 us
  waiting for transfers between devices  250 us (63%)
  blocking collectives  87.2 us (22%)
  matrix products  32.3 us (8%)
  between operations  14.7 us (4%)
  local copies, waits for them, and re-layouts  7.4 us (2%)
  other arithmetic  6.04 us (2%)
    reduce_scatter x1, waiting for transfers between devices, shards(): lax.psum_scatter(lax.dot_general(mixed, basis_block, (((0,), (1,)), ((),...  136 us
    psum x1, blocking collectives, shards(): rotated_out = lax.psum(partial_out, ('tp', 'row')).astype(jnp.bfloat16)  85.1 us
    all_gather x1, waiting for transfers between devices, shards(): mixed = lax.all_gather(mixed, 'row', axis=0, tiled=True)  83.2 us
    all_gather x1, waiting for transfers between devices, shards(): basis_block = lax.all_gather(basis_in, 'col', axis=0, tiled=True)  22.6 us
    dot_general x1, matrix products, shards(): lax.dot_general(mixed, basis_block, (((0,), (1,)), ((), ())), preferred_e...  22 us
  transfers between devices with their start and end apart: 6, of which 4 were waited for; matrix products, arithmetic and copies ran while one was open for 0% of the time, Pallas kernels for 0%

commit v1 on v0

--- a/solution.py
+++ b/solution.py
@@ -29,7 +29,7 @@
     rotated_in = lax.all_gather(rotated_in, "col", axis=0, tiled=True)
     queries = rotated_in.shape[0]
     partial_out = jnp.dot(out_grad, basis_out, preferred_element_type=jnp.float32)
-    rotated_out = lax.psum(partial_out, ("tp", "row")).astype(jnp.bfloat16)
+    rotated_out = lax.psum(lax.psum(partial_out, "tp"), "row").astype(jnp.bfloat16)
     coeff = contract_rows(rotated_in, rotated_out)
     scaled = (coeff / (queries * (eigen + damping))).astype(jnp.bfloat16)
     mixed_part = contract_cols(scaled, lax.all_gather(basis_out, ("tp", "row"), axis=0, tiled=True))

time: 398 us -> 412 us (1.035)
  waiting for transfers between devices: 250 us -> 321 us
  blocking collectives: 87.2 us -> 27.7 us
    psum x1, blocking collectives: 85.1 us -> 25.6 us  [shards(): lax.psum(lax.psum(partial_out, 'tp'), 'row').astype(jnp.bfloat16)]
    all_gather x1, waiting for transfers between devices: 0.01 us -> 51.4 us  [shards(): lax.all_gather(basis_out, ('tp', 'row'), axis=0, tiled=True)]
    psum x0 -> x1, waiting for transfers between devices: none -> 20.2 us  [shards(): lax.psum(partial_out, 'tp')]
  transfers between devices with their start and end apart: 6 -> 7, of which waited for: 4 -> 6; matrix products, arithmetic and copies ran while one was open for 0% -> 2% of each run, Pallas kernels for 0% -> 0%
where the time goes in v1:
time: 412 us; the launch traced here: 411 us
  waiting for transfers between devices  321 us (78%)
  matrix products  34 us (8%)
  blocking collectives  27.7 us (7%)
  between operations  14.9 us (4%)
  local copies, waits for them, and re-layouts  7.4 us (2%)
  other arithmetic  6.04 us (1%)
    reduce_scatter x1, waiting for transfers between devices, shards(): lax.psum_scatter(lax.dot_general(mixed, basis_block, (((0,), (1,)), ((),...  136 us
    all_gather x1, waiting for transfers between devices, shards(): mixed = lax.all_gather(mixed, 'row', axis=0, tiled=True)  83.2 us
    all_gather x1, waiting for transfers between devices, shards(): lax.all_gather(basis_out, ('tp', 'row'), axis=0, tiled=True)  51.4 us
    psum x1, blocking collectives, shards(): lax.psum(lax.psum(partial_out, 'tp'), 'row').astype(jnp.bfloat16)  25.6 us
    dot_general x1, matrix products, shards(): lax.dot_general(mixed, basis_block, (((0,), (1,)), ((), ())), preferred_e...  22 us
    all_gather x1, waiting for transfers between devices, shards(): basis_block = lax.all_gather(basis_in, 'col', axis=0, tiled=True)  20.7 us
    psum x1, waiting for transfers between devices, shards(): lax.psum(partial_out, 'tp')  20.2 us
    reduce_scatter x1, waiting for transfers between devices, shards(): lax.psum_scatter(mixed_part.astype(jnp.bfloat16), 'col', scatter_dimensio...  8.47 us
  transfers between devices with their start and end apart: 7, of which 6 were waited for; matrix products, arithmetic and copies ran while one was open for 2% of the time, Pallas kernels for 0%

profile of v1, /device:TPU:0, one launch (start us, length us, event | category | flops | bytes accessed | tf_op | source)
XLA Modules:
  0.0 411.4 jit_solution(9068211041737583419)
XLA Ops:
  7.4 0.7 all-gather.4.cloned.1.call-update
  8.1 0.0 all-reduce.3.cloned.1.call-start
  8.1 1.9 fusion.9
  10.1 0.0 reduce-scatter.4.cloned.1.call-start
  10.1 20.7 %all-gather.4.cloned.1.call-done = bf16[3584,1024]{1,0:T(8,128)(2,1)} async-done(((bf16[1792,1024]{1,0:T(8,128)(2,1)}), bf16[3584,1024]{1,0:T(8,128)(2,1)}) %all-gather.4.cloned.1.call-update) | async-done | bytes 7340048 | tf_op jit(solution)/shard_map/all_gather | solution.py:24
  30.8 5.1 %convolution_convert_fusion.2 = bf16[64,1024]{1,0:T(8,128)(2,1)} fusion(bf16[64,3584]{1,0:T(8,128)(2,1)S(1)} %copy-done, bf16[3584,1024]{1,0:T(8,128)(2,1)} %all-gather.4.cloned.1.call-done), kind=kOutput, calls=%fused_computation.4 | convolution fusion | flops 469827584 | bytes 7929856 | tf_op jit(solution)/shard_map/dot_general | solution.py:25
  35.9 0.0 all-gather.6.cloned.1.call-start
  36.0 0.5 all-gather.6.cloned.1.call-update
  36.5 0.0 reduce-scatter.6.cloned.1.call-start
  36.6 20.2 %all-reduce.3.cloned.1.call-done = f32[128,512]{1,0:T(8,128)} async-done(((f32[128,512]{1,0:T(8,128)}), f32[128,512]{1,0:T(8,128)}) %all-reduce.3.cloned.1.call-update) | async-done | bytes 262160 | tf_op jit(solution)/shard_map/psum | solution.py:32
  56.7 25.6 %all-reduce.4 = bf16[128,512]{1,0:T(8,128)(2,1)S(1)} all-reduce(f32[128,512]{1,0:T(8,128)} %all-reduce.3.cloned.1.call-done), channel_id=1, replica_groups=mesh['tp'=4,'row'=4,'col'=2] {'row'}, use_global_device_ids=true, to_apply=%region_2.0 | all-reduce | flops 65536 | bytes 393216 | tf_op jit(solution)/shard_map/psum | solution.py:32
  82.3 0.0 reduce-scatter.4.cloned.1.call-done
  82.4 2.1 all_gather.13
  84.4 51.4 %all-gather.6.cloned.1.call-done = bf16[4096,512]{1,0:T(8,128)(2,1)} async-done(((bf16[256,512]{1,0:T(8,128)(2,1)}), bf16[4096,512]{1,0:T(8,128)(2,1)}) %all-gather.6.cloned.1.call-update) | async-done | bytes 4194320 | tf_op jit(solution)/shard_map/all_gather | solution.py:35
  135.9 4.9 %convolution_convert_fusion.1 = bf16[256,4096]{1,0:T(8,128)(2,1)} fusion(bf16[4096,512]{1,0:T(8,128)(2,1)} %all-gather.6.cloned.1.call-done, bf16[128,256]{1,0:T(8,128)(2,1)S(1)} %all_gather.13, f32[256,512]{1,0:T(8,128)S(1)} %copy-done.1, bf16[128,512]{1,0:T(8,128)(2,1)S(1)} %all-reduce.4), kind=kOutput, calls=%fused_computation.1 | convolution fusion | flops 1108869120 | bytes 7012352 | tf_op jit(solution)/shard_map/dot_general | solution.py:16
  140.8 3.3 convert_element_type.30
  144.1 4.1 copy.6
  148.2 0.0 all-gather.8.cloned.1.call-start
  148.3 8.5 %reduce-scatter.6.cloned.1.call-done = bf16[256,4,1,512]{0,3,1,2:T(8,128)(2,1)} async-done(((bf16[256,4,2,512]{0,3,1,2:T(8,128)(2,1)}), bf16[256,4,1,512]{0,3,1,2:T(8,128)(2,1)}) %reduce-scatter.6.cloned.1.call-update) | async-done | bytes 1048592 | tf_op jit(solution)/shard_map/reduce_scatter | solution.py:39
  156.8 0.0 reduce-scatter.8.cloned.1.call-start
  156.8 83.2 %all-gather.8.cloned.1.call-done = bf16[1024,2048]{0,1:T(8,128)(2,1)} async-done(((bf16[256,2048]{0,1:T(8,128)(2,1)}), bf16[1024,2048]{0,1:T(8,128)(2,1)}) %all-gather.8.cloned.1.call-update) | async-done | bytes 4194320 | tf_op jit(solution)/shard_map/all_gather | solution.py:43
  240.0 22.0 %convolution_convert_fusion = bf16[2048,3584]{1,0:T(8,128)(2,1)} fusion(bf16[1024,2048]{0,1:T(8,128)(2,1)} %all-gather.8.cloned.1.call-done, bf16[3584,1024]{1,0:T(8,128)(2,1)} %all-gather.4.cloned.1.call-done), kind=kOutput, calls=%fused_computation | convolution fusion | flops 15039725568 | bytes 26214400 | tf_op jit(solution)/shard_map/dot_general | solution.py:45
  262.1 135.9 %reduce-scatter.8.cloned.1.call-done = bf16[512,3584]{1,0:T(8,128)(2,1)} async-done(((bf16[2048,3584]{1,0:T(8,128)(2,1)}), bf16[512,3584]{1,0:T(8,128)(2,1)}) %reduce-scatter.8.cloned.1.call-update) | async-done | bytes 3670032 | tf_op jit(solution)/shard_map/reduce_scatter | solution.py:44
  398.0 6.0 %convert_element_type.33 = f32[512,3584]{1,0:T(8,128)} convert(bf16[512,3584]{1,0:T(8,128)(2,1)} %reduce-scatter.8.cloned.1.call-done) | non-fusion elementwise | flops 1835008 | bytes 11010048 | tf_op jit(solution)/shard_map/convert_element_type | solution.py:51
  (10 shorter events, 0.1 us)
Async XLA Ops:
  7.4 23.4 %copy-start = (bf16[64,3584]{1,0:T(8,128)(2,1)S(1)}, bf16[64,3584]{1,0:T(8,128)(2,1)}, u32[]{:S(2)}) copy-start(bf16[64,3584]{1,0:T(8,128)(2,1)} %param.5) | copy-start | bytes 1376260
  7.4 23.4 %all-gather.4.cloned.1.call-start = ((), (), s32[]{:S(2)}) async-start(), calls=%async_computation.3 | async-start | bytes 11010048 | tf_op jit(solution)/shard_map/all_gather | solution.py:24
  8.1 48.7 %all-reduce.3.cloned.1.call-start = ((), (), s32[]{:S(2)}) async-start(), calls=%async_computation.5 | async-start | bytes 524288 | tf_op jit(solution)/shard_map/psum | solution.py:32
  10.0 125.8 %copy-start.1 = (f32[256,512]{1,0:T(8,128)S(1)}, f32[256,512]{1,0:T(8,128)}, u32[]{:S(2)}) copy-start(f32[256,512]{1,0:T(8,128)} %param.9) | copy-start | bytes 1572868
  10.1 72.3 %reduce-scatter.4.cloned.1.call-start = ((), (), s32[]{:S(2)}) async-start(), calls=%async_computation.4 | async-start | bytes 163840 | tf_op jit(solution)/shard_map/reduce_scatter | solution.py:26
  35.9 100.0 %all-gather.6.cloned.1.call-start = ((), (), s32[]{:S(2)}) async-start(), calls=%async_computation.6 | async-start | bytes 4456448 | tf_op jit(solution)/shard_map/all_gather | solution.py:35
  36.5 120.2 %reduce-scatter.6.cloned.1.call-start = ((), (), s32[]{:S(2)}) async-start(), calls=%async_computation.7 | async-start | bytes 3145728 | tf_op jit(solution)/shard_map/reduce_scatter | solution.py:39
  148.2 91.8 %all-gather.8.cloned.1.call-start = ((), (), s32[]{:S(2)}) async-start(), calls=%async_computation.8 | async-start | bytes 5242880 | tf_op jit(solution)/shard_map/all_gather | solution.py:43
  156.8 241.2 %reduce-scatter.8.cloned.1.call-start = ((), (), s32[]{:S(2)}) async-start(), calls=%async_computation.9 | async-start | bytes 18350080 | tf_op jit(solution)/shard_map/reduce_scatter | solution.py:44
Sparse Core Ops, SparseCore 0:
  9.7 21.0 all-gather.3
  36.1 20.6 reduce-scatter.3
  148.4 8.3 reduce-scatter.5
  158.2 81.8 all-gather.7
Sparse Core Ops, SparseCore 1:
  11.5 45.2 all-reduce.2
  59.4 76.5 all-gather.5
  262.1 135.8 reduce-scatter.7
